TPU v7x, 32 devices: a whole 2x2x4 slice. The times are simulated.
32 devices in a mesh: view: 8 (over z, x), head: 4 (over y, core).
Axes of the slice: x: 2, y: 2, z: 4, core: 2. Of those that a mesh axis runs over, the one named last changes fastest.
Arguments:
- features: bfloat16 [16384, 1024], P(('view', 'head')), may hold values from -6 to 6
- attend_weight: bfloat16 [2, 3, 1024, 1024], P(None, None, 'view', 'head'), may hold values from -0.1875 to 0.1875
- output_weight: bfloat16 [2, 1024, 1024], P(None, 'view'), may hold values from -0.1875 to 0.1875
- fast_init: bfloat16 [2, 16, 3, 64, 512], P(None, 'head', None, None, 'view'), may hold values from -0.75 to 0.75
- update_mask: int32 [8, 2048], P('view'), may hold values 0 or 1
Outputs:
- refined: bfloat16 [16384, 1024], P(('view', 'head'))
All inputs are finite; a program needn't handle non-finite values. No bound on the sum of `update_mask` on one device may be relied on, other than what follows from the above.
Results may differ from a plain program's by a relative error of at most 0.035.
Values may be sent and summed in bfloat16 or wider, within the bound.
No kernel may reach another device: no remote copies, remote signals or barrier semaphores. Data moves between devices by JAX's collectives and lax.ppermute only.
A program may use at most 64 MiB of HBM per device.

v0:
```python
import jax
import jax.numpy as jnp
from jax import lax
from jax.sharding import PartitionSpec as P

BLOCKS = 2
NS_STEPS = 5
newton_coeffs = (3.4445, -4.775, 2.0315)
learn_rate = 1.0
score_scale = 0.25


def normalize(values, epsilon):
    return values * lax.rsqrt(jnp.mean(values * values, axis=-1, keepdims=True) + epsilon)


def newton_step(current, gram_matrix):
    squared = jnp.einsum(
        "...de,...ef->...df", gram_matrix, gram_matrix, precision=lax.Precision.HIGHEST
    )
    polynomial = newton_coeffs[1] * gram_matrix + newton_coeffs[2] * squared
    return newton_coeffs[0] * current + jnp.einsum(
        "...de,...ef->...df", polynomial, current, precision=lax.Precision.HIGHEST
    )


def self_gram(current):
    return jnp.einsum("...df,...ef->...de", current, current, precision=lax.Precision.HIGHEST)


def fast_gradient(keys, values, mask, weights):
    first = jnp.einsum("thd,hdf->thf", keys, weights[:, 0], preferred_element_type=jnp.float32)
    third = jnp.einsum("thd,hdf->thf", keys, weights[:, 1], preferred_element_type=jnp.float32)
    sigma = jax.nn.sigmoid(first)
    hidden = (first * sigma * third).astype(jnp.bfloat16)
    target = (-(mask[:, None, None].astype(jnp.float32) * values.astype(jnp.float32))).astype(
        jnp.bfloat16
    )
    back = jnp.einsum("thd,hdf->thf", target, weights[:, 2], preferred_element_type=jnp.float32)
    d_third = (back * first * sigma).astype(jnp.bfloat16)
    d_first = (back * third * sigma * (1.0 + first * (1.0 - sigma))).astype(jnp.bfloat16)
    grad_first = jnp.einsum("thd,thf->hdf", keys, d_first, preferred_element_type=jnp.float32)
    grad_third = jnp.einsum("thd,thf->hdf", keys, d_third, preferred_element_type=jnp.float32)
    grad_last = jnp.einsum("thd,thf->hdf", target, hidden, preferred_element_type=jnp.float32)
    return jnp.stack([grad_first, grad_third, grad_last], axis=1)


def fast_apply(queries, weights):
    first = jnp.einsum("thd,hdf->thf", queries, weights[:, 0], preferred_element_type=jnp.float32)
    third = jnp.einsum("thd,hdf->thf", queries, weights[:, 1], preferred_element_type=jnp.float32)
    hidden = (first * jax.nn.sigmoid(first) * third).astype(jnp.bfloat16)
    output = jnp.einsum("thf,hdf->thd", hidden, weights[:, 2], preferred_element_type=jnp.float32)
    return normalize(output, 1e-05)


def shards(features, attend_weight, output_weight, fast_init, update_mask):
    stream = features
    view_dev, view_len = update_mask.shape
    heads_here = fast_init.shape[1]
    head_dim = fast_init.shape[3]
    rows_all = view_dev * view_len
    block = min(512, view_len)
    count = rows_all // block
    mask_blocks = update_mask.reshape(count, block)
    for layer in range(BLOCKS):
        normed = normalize(stream.astype(jnp.float32), 1e-05).astype(jnp.bfloat16)
        whole = lax.all_gather(normed, "head", axis=0, tiled=True)
        packed = jnp.einsum(
            "td,jdc->tjc",
            whole,
            lax.all_gather(attend_weight[layer], "view", axis=1, tiled=True),
            preferred_element_type=jnp.float32,
        ).astype(jnp.bfloat16)
        packed = packed.reshape(rows_all, 3, heads_here, head_dim)
        queries = normalize(packed[:, 0].astype(jnp.float32), 1e-05).astype(jnp.bfloat16)
        keys = normalize(packed[:, 1].astype(jnp.float32), 1e-05).astype(jnp.bfloat16)
        values = packed[:, 2]
        key_views = keys.reshape(view_dev, view_len, heads_here, head_dim)
        value_views = values.reshape(view_dev, view_len, heads_here, head_dim)
        query_blocks = jnp.moveaxis(
            queries.reshape(view_dev, view_len // block, block, heads_here, head_dim), 1, 0
        )

        def attend_block(query_block):
            scores = (
                jnp.einsum(
                    "vqhd,vkhd->vhqk", query_block, key_views, preferred_element_type=jnp.float32
                )
                * score_scale
            )
            expo = jnp.exp(scores)
            probs = (expo / jnp.sum(expo, axis=-1, keepdims=True)).astype(jnp.bfloat16)
            return jnp.einsum(
                "vhqk,vkhd->vqhd", probs, value_views, preferred_element_type=jnp.float32
            )

        attended = jnp.moveaxis(lax.map(attend_block, query_blocks), 0, 1).reshape(
            rows_all, heads_here, head_dim
        )
        local_fast = fast_init[layer]
        full_fast = lax.all_gather(local_fast, "view", axis=3, tiled=True)

        def accumulate(total, inputs):
            return (total + fast_gradient(inputs[0], inputs[1], inputs[2], full_fast), None)

        key_blocks = keys.reshape(count, block, heads_here, head_dim)
        value_blocks = values.reshape(count, block, heads_here, head_dim)
        gradients, _ = lax.scan(
            accumulate,
            jnp.zeros(full_fast.shape, jnp.float32),
            (key_blocks, value_blocks, mask_blocks),
        )
        summed = lax.psum(gradients.astype(jnp.bfloat16), "view").astype(jnp.float32)
        squares = jnp.sum(summed * summed, axis=(2, 3), keepdims=True)
        current = summed * lax.rsqrt(squares + 1e-06)
        for _ in range(NS_STEPS):
            current = newton_step(current, self_gram(current))
        updated = (full_fast.astype(jnp.float32) - learn_rate * current).astype(jnp.bfloat16)

        def apply_block(query_block):
            return fast_apply(query_block, updated)

        applied = lax.map(apply_block, queries.reshape(count, block, heads_here, head_dim)).reshape(
            rows_all, heads_here, head_dim
        )
        mixed = (attended + applied).astype(jnp.bfloat16).reshape(rows_all, heads_here * head_dim)
        regrouped = lax.all_to_all(mixed, "head", split_axis=0, concat_axis=1, tiled=True)
        projected = jnp.dot(
            regrouped,
            lax.all_gather(output_weight[layer], "view", axis=0, tiled=True),
            preferred_element_type=jnp.float32,
        )
        stream = (stream.astype(jnp.float32) + projected).astype(jnp.bfloat16)
    return stream


def solution(mesh):
    return jax.shard_map(
        shards,
        mesh=mesh,
        in_specs=(
            P(("view", "head"), None),
            P(None, None, "view", "head"),
            P(None, "view", None),
            P(None, "head", None, None, "view"),
            P("view", None),
        ),
        out_specs=P(("view", "head"), None),
        check_vma=False,
    )
```

profile of v0, /device:TPU:0, one launch (start us, length us, event | category | flops | bytes accessed | tf_op | source)
XLA Modules:
  0.0 636.8 jit_solution(1773703120889669409)
XLA Ops:
  11.7 44.0 %all-gather.1 = bf16[1,4,3,64,512]{3,1,2,0,4:T(4,128)(2,1)} all-gather(bf16[1,4,3,64,64]{3,1,2,0,4:T(4,128)(2,1)S(1)} %copy.61), channel_id=3, replica_groups=mesh['view'=8,'head'=4] {'view'}, dimensions={4}, use_global_device_ids=true | all-gather | bytes 884736 | tf_op jit(solution)/shard_map/all_gather | solution.py:101
  59.5 6.3 all-gather.17.cloned.1.call-done
  65.8 35.9 %all-gather.13.cloned.1.call-done = bf16[2048,1024]{1,0:T(8,128)(2,1)} async-done(((bf16[512,1024]{1,0:T(8,128)(2,1)}), bf16[2048,1024]{1,0:T(8,128)(2,1)}) %all-gather.13.cloned.1.call-update) | async-done | bytes 4194320 | tf_op jit(solution)/shard_map/all_gather | solution.py:67
  101.7 6.1 fusion.188
  111.3 3.7 reshape.323
  122.1 60.1 %while.66 = (s32[]{:T(128)}, f32[4,3,64,512]{3,2,0,1:T(8,128)S(1)}, bf16[4,512,4,64]{1,3,2,0:T(8,128)(2,1)}, s32[4,512]{1,0:T(4,128)S(1)}, bf16[4,512,4,64]{1,3,...) while((s32[]{:T(128)}, f32[4,3,64,512]{3,2,0,1:T(8,128)S(1)}, ...), condition=%wide.region_7.8_spmd.clone, body=%wide.region_6.7_spmd.clone.sunk | while | flops 830996992 | bytes 50605152 | solution.py:108
  199.0 31.0 %while.62 = (s32[]{:T(128)}, f32[4,1,512,4,64]{2,4,3,1,0:T(8,128)S(1)}, bf16[4,1,512,4,64]{2,4,3,1,0:T(8,128)(2,1)}, bf16[1,2048,4,64]{1,3,2,0:T(8,128)(2,1)S(1)}, bf16[1,2048,4,64]{1,3,2,0:T(8,128)(2,1)}, /*index=5*/s32[]{:T(128)}) while((s32[]{:T(128)}, f32[4,1,512,4,64]{2,4,3,1,0:T(8,128)S(1)}, bf16[4,1,512,4,64]{2,4,3,1,0:T(8,128)(2,1)}, ...), condition=%wide.region_5.6_spmd, body=%wide.region_3.5_spmd.sunk | while | flops 1094711296 | bytes 40649316 | solution.py:97
  199.0 4.0 fusion.368
  206.8 4.0 fusion.368
  214.6 4.0 fusion.368
  222.3 4.0 fusion.368
  226.4 3.7 fusion.369
  230.0 28.5 %all-reduce.3.cloned.1.call-done = bf16[4,3,64,512]{3,2,1,0:T(8,128)(2,1)} async-done(((bf16[4,3,64,512]{3,2,1,0:T(8,128)(2,1)}), bf16[4,3,64,512]{3,2,1,0:T(8,128)(2,1)}) %all-reduce.3.cloned.1.call-update) | async-done | bytes 786448 | tf_op jit(solution)/shard_map/psum | solution.py:113
  283.2 35.3 %while.63 = (s32[]{:T(128)}, f32[4,512,4,64]{1,3,2,0:T(8,128)}, bf16[4,512,4,64]{1,3,2,0:T(8,128)(2,1)}, bf16[4,3,64,512]{3,2,0,1:T(8,128)(2,1)}, s32[]{:T(128)}) while((s32[]{:T(128)}, f32[4,512,4,64]{1,3,2,0:T(8,128)}, bf16[4,512,4,64]{1,3,2,0:T(8,128)(2,1)}, bf16[4,3,64,512]{3,2,0,1:T(8,128)(2,1)}, s32[]{:T(128)}) %tuple.131), condition=%wide.region_12.13_spmd, body=%wide.region_10.12_spmd.sunk | while | flops 409339904 | bytes 11306557 | solution.py:123
  283.2 3.8 fusion.374
  287.0 4.1 multiply_reduce_fusion.8
  292.0 3.8 fusion.374
  295.8 4.2 multiply_reduce_fusion.8
  300.8 3.8 fusion.374
  304.6 4.1 multiply_reduce_fusion.8
  309.7 3.8 fusion.374
  313.4 4.2 multiply_reduce_fusion.8
  325.1 14.3 %all-to-all-done = bf16[4,512,256]{1,2,0:T(8,128)(2,1)S(1)} async-done(((bf16[4,512,256]{1,2,0:T(8,128)(2,1)}), bf16[4,512,256]{1,2,0:T(8,128)(2,1)S(1)}, u32[]{:S(2)}, u32[]{:S(2)}) %all-to-all-start) | async-done | bytes 1048608 | tf_op jit(solution)/shard_map/all_to_all | solution.py:127
  344.9 38.5 %all-gather.4 = bf16[1,4,3,64,512]{3,1,2,0,4:T(4,128)(2,1)} all-gather(bf16[1,4,3,64,64]{3,1,2,0,4:T(4,128)(2,1)S(1)} %copy.63), channel_id=6, replica_groups=mesh['view'=8,'head'=4] {'view'}, dimensions={4}, use_global_device_ids=true | all-gather | bytes 884736 | tf_op jit(solution)/shard_map/all_gather | solution.py:101
  386.2 5.2 all-gather.15.cloned.1.call-done
  391.5 6.1 fusion.191
  411.8 62.9 %while.67 = (s32[]{:T(128)}, f32[4,3,64,512]{3,2,0,1:T(8,128)S(1)}, bf16[4,512,4,64]{1,3,2,0:T(8,128)(2,1)}, s32[4,512]{1,0:T(4,128)}, bf16[4,512,4,64]{1,3,2,0:...) while((s32[]{:T(128)}, f32[4,3,64,512]{3,2,0,1:T(8,128)S(1)}, ...), condition=%wide.region_20.21_spmd.clone, body=%wide.region_19.20_spmd.clone.sunk | while | flops 830996992 | bytes 50605152 | solution.py:108
  491.3 34.0 %while.64 = (s32[]{:T(128)}, f32[4,1,512,4,64]{2,4,3,1,0:T(8,128)}, bf16[4,1,512,4,64]{2,4,3,1,0:T(8,128)(2,1)}, bf16[1,2048,4,64]{1,3,2,0:T(8,128)(2,1)S(1)}, bf16[1,2048,4,64]{1,3,2,0:T(8,128)(2,1)}, /*index=5*/s32[]{:T(128)}) while((s32[]{:T(128)}, f32[4,1,512,4,64]{2,4,3,1,0:T(8,128)}, bf16[4,1,512,4,64]{2,4,3,1,0:T(8,128)(2,1)}, ...), condition=%wide.region_18.19_spmd, body=%wide.region_16.18_spmd.sunk | while | flops 1094711296 | bytes 40649824 | solution.py:97
  491.3 4.1 fusion.376
  495.4 4.3 fusion.377
  499.7 4.0 fusion.376
  503.8 4.3 fusion.377
  508.1 4.0 fusion.376
  512.2 4.3 fusion.377
  516.5 4.0 fusion.376
  520.5 4.3 fusion.377
  526.9 24.3 %all-reduce.5.cloned.1.call-done = bf16[4,3,64,512]{3,2,1,0:T(8,128)(2,1)} async-done(((bf16[4,3,64,512]{3,2,1,0:T(8,128)(2,1)}), bf16[4,3,64,512]{3,2,1,0:T(8,128)(2,1)}) %all-reduce.5.cloned.1.call-update) | async-done | bytes 786448 | tf_op jit(solution)/shard_map/psum | solution.py:113
  573.2 31.6 %while.65 = (s32[]{:T(128)}, f32[4,512,4,64]{1,3,2,0:T(8,128)S(1)}, bf16[4,512,4,64]{1,3,2,0:T(8,128)(2,1)}, bf16[4,3,64,512]{3,2,0,1:T(8,128)(2,1)S(1)}, s32[]{:T(128)}) while((s32[]{:T(128)}, f32[4,512,4,64]{1,3,2,0:T(8,128)S(1)}, bf16[4,512,4,64]{1,3,2,0:T(8,128)(2,1)}, bf16[4,3,64,512]{3,2,0,1:T(8,128)(2,1)S(1)}, s32[]{:T(128)}) %tuple.140), condition=%wide.region_25.26_spmd, body=%wide.region_23.25_spmd.sunk | while | flops 409339904 | bytes 11306049 | solution.py:123
  573.2 3.7 fusion.382
  576.9 4.1 multiply_reduce_fusion.9
  581.1 3.7 fusion.382
  584.8 4.1 multiply_reduce_fusion.9
  589.0 3.7 fusion.382
  592.7 4.1 multiply_reduce_fusion.9
  596.9 3.7 fusion.382
  600.6 4.1 multiply_reduce_fusion.9
  611.6 14.4 %all-to-all-done.1 = bf16[4,512,256]{1,2,0:T(8,128)(2,1)S(1)} async-done(((bf16[4,512,256]{1,2,0:T(8,128)(2,1)}), bf16[4,512,256]{1,2,0:T(8,128)(2,1)S(1)}, u32[]{:S(2)}, u32[]{:S(2)}) %all-to-all-start.1) | async-done | bytes 1048608 | tf_op jit(solution)/shard_map/all_to_all | solution.py:127
  625.9 3.8 fusion.199
  (260 shorter events, 273.8 us)
Async XLA Ops:
  6.5 2.7 copy-start.7
  6.5 59.3 %all-gather.17.cloned.1.call-start = ((), (), s32[]{:S(2)}) async-start(), calls=%async_computation.6 | async-start | bytes 1769472 | tf_op jit(solution)/shard_map/all_gather | solution.py:71
  9.2 1.7 copy-start.20
  9.2 92.5 %all-gather.13.cloned.1.call-start = ((), (), s32[]{:S(2)}) async-start(), calls=%async_computation.2 | async-start | bytes 5242880 | tf_op jit(solution)/shard_map/all_gather | solution.py:67
  10.8 247.8 %all-reduce.3.cloned.1.call-start = ((), (), s32[]{:S(2)}) async-start(), calls=%async_computation.3 | async-start | bytes 1572864 | tf_op jit(solution)/shard_map/psum | solution.py:113
  11.7 47.1 %copy-start.22 = (s32[1,2048]{1,0:T(1,128)S(1)}, s32[1,2048]{1,0:T(1,128)}, u32[]{:S(2)}) copy-start(s32[1,2048]{1,0:T(1,128)} %param.21) | copy-start | bytes 24580
  107.9 3.3 copy-start.2
  182.2 2.0 copy-start.21
  182.2 1.1 copy-start.19
  182.3 2.2 copy-start.18
  183.3 5.4 copy-start
  183.3 141.8 %all-gather.19.cloned.1.call-start = ((), (), s32[]{:S(2)}) async-start(), calls=%async_computation.7 | async-start | bytes 2359296 | tf_op jit(solution)/shard_map/all_gather | solution.py:130
  184.3 202.0 %all-gather.21.cloned.1.call-start = ((), (), s32[]{:S(2)}) async-start(), calls=%async_computation.8 | async-start | bytes 1769472 | tf_op jit(solution)/shard_map/all_gather | solution.py:71
  193.6 1.9 copy-start.6
  195.5 1.6 copy-start.5
  199.0 4.1 copy-start.13
  206.8 4.1 copy-start.13
  214.5 4.1 copy-start.13
  222.3 4.1 copy-start.13
  258.6 5.3 copy-start.11
  276.9 2.1 copy-start.9
  321.4 18.1 %copy-start.8 = (bf16[512,1024]{1,0:T(8,128)(2,1)S(1)}, bf16[512,1024]{1,0:T(8,128)(2,1)}, u32[]{:S(2)}) copy-start(bf16[512,1024]{1,0:T(8,128)(2,1)} %param.17) | copy-start | bytes 3145732
  321.4 18.1 %all-to-all-start = ((bf16[4,512,256]{1,2,0:T(8,128)(2,1)}), bf16[4,512,256]{1,2,0:T(8,128)(2,1)S(1)}, u32[]{:S(2)}, u32[]{:S(2)}) async-start(bf16[4,512,256]{1,2,0:T(8,128)(2,1)} %fusion.206), calls=%async_computation | async-start | bytes 2097152 | tf_op jit(solution)/shard_map/all_to_all | solution.py:127
  325.1 66.4 %all-gather.15.cloned.1.call-start = ((), (), s32[]{:S(2)}) async-start(), calls=%async_computation.4 | async-start | bytes 5242880 | tf_op jit(solution)/shard_map/all_gather | solution.py:67
  342.4 1.0 copy-start.15
  342.4 2.3 copy-start.17
  344.7 206.5 %all-reduce.5.cloned.1.call-start = ((), (), s32[]{:S(2)}) async-start(), calls=%async_computation.5 | async-start | bytes 1572864 | tf_op jit(solution)/shard_map/psum | solution.py:113
  397.6 3.3 copy-start.3
  475.8 135.8 %all-gather.23.cloned.1.call-start = ((), (), s32[]{:S(2)}) async-start(), calls=%async_computation.9 | async-start | bytes 2359296 | tf_op jit(solution)/shard_map/all_gather | solution.py:130
  476.5 5.1 copy-start.1
  491.3 34.0 %copy-start.4 = (f32[4,512,4,64]{1,0,3,2:T(4,128)S(1)}, f32[4,512,4,64]{1,0,3,2:T(4,128)}, u32[]{:S(2)}) copy-start(f32[4,512,4,64]{1,0,3,2:T(4,128)} %reshape.326) | copy-start | bytes 6291460
  491.3 4.1 copy-start.14
  499.7 4.0 copy-start.14
  508.1 4.0 copy-start.14
  516.5 4.0 copy-start.14
  551.1 5.2 copy-start.12
  569.1 2.1 copy-start.10
  607.9 18.1 %copy-start.16 = (bf16[512,1024]{1,0:T(8,128)(2,1)S(1)}, bf16[512,1024]{1,0:T(8,128)(2,1)}, u32[]{:S(2)}) copy-start(bf16[512,1024]{1,0:T(8,128)(2,1)} %copy-done.15) | copy-start | bytes 3145732
  607.9 18.1 %all-to-all-start.1 = ((bf16[4,512,256]{1,2,0:T(8,128)(2,1)}), bf16[4,512,256]{1,2,0:T(8,128)(2,1)S(1)}, u32[]{:S(2)}, u32[]{:S(2)}) async-start(bf16[4,512,256]{1,2,0:T(8,128)(2,1)} %fusion.202), calls=%async_computation.1 | async-start | bytes 2097152 | tf_op jit(solution)/shard_map/all_to_all | solution.py:127
Sparse Core Ops, SparseCore 0:
  9.4 56.3 all-gather.16
  67.4 34.3 all-gather.12
  183.4 75.1 all-reduce.2
  260.6 48.2 all-gather.18
  310.8 45.6 all-gather.20
  357.8 33.5 all-gather.14
  475.9 75.2 all-reduce.4
  553.2 48.2 all-gather.22
where the time goes:
time: 649 us; the launch traced here: 637 us
  matrix products  294 us (45%)
  waiting for transfers between devices  130 us (20%)
  blocking collectives  82.5 us (13%)
  local copies, waits for them, and re-layouts  56.3 us (9%)
  other arithmetic  50.9 us (8%)
  between operations  14.3 us (2%)
  starting transfers between devices  7.77 us (1%)
    all_gather x2, blocking collectives, shards(): full_fast = lax.all_gather(local_fast, 'view', axis=3, tiled=True)  82.5 us
    psum x2, waiting for transfers between devices, shards(): lax.psum(gradients.astype(jnp.bfloat16), 'view').astype(jnp.float32)  52.8 us
    all_gather x2, waiting for transfers between devices, shards(): whole = lax.all_gather(normed, 'head', axis=0, tiled=True)  41.2 us
    dot_general x8, matrix products, fast_apply(): jnp.einsum('thf,hdf->thd', hidden, weights[:, 2], preferred_element_type=...  33 us
    dot_general x8, matrix products, attend_block(): jnp.einsum('vqhd,vkhd->vhqk', query_block, key_views, preferred_element_t...  32.4 us
    dot_general x8, matrix products, attend_block(): jnp.einsum('vhqk,vkhd->vqhd', probs, value_views, preferred_element_type=...  31.9 us
    dot_general x8, matrix products, fast_apply(): jnp.einsum('thd,hdf->thf', queries, weights[:, 0], preferred_element_type...  29.9 us
    all_to_all x2, waiting for transfers between devices, shards(): lax.all_to_all(mixed, 'head', split_axis=0, concat_axis=1, tiled=True)  28.7 us
  transfers between devices with their start and end apart: 10, of which 7 were waited for; matrix products, arithmetic and copies ran while one was open for 36% of the time, Pallas kernels for 0%

commit v1 on v0

--- a/solution.py
+++ b/solution.py
@@ -64,7 +64,14 @@
     mask_blocks = update_mask.reshape(count, block)
     for layer in range(BLOCKS):
         normed = normalize(stream.astype(jnp.float32), 1e-05).astype(jnp.bfloat16)
-        whole = lax.all_gather(normed, "head", axis=0, tiled=True)
+        ring = [normed]
+        for hop in range(3):
+            ring.append(lax.ppermute(ring[-1], "head", [(dev, (dev + 1) % 4) for dev in range(4)]))
+        whole = jnp.roll(
+            jnp.concatenate(ring[::-1], axis=0),
+            (lax.axis_index("head") + 1) * ring[0].shape[0],
+            axis=0,
+        )
         packed = jnp.einsum(
             "td,jdc->tjc",
             whole,

time: 649 us -> 665 us (1.025)
  matrix products: 294 us -> 309 us
    ppermute x0 -> x6, waiting for transfers between devices: none -> 54.8 us  [shards(): lax.ppermute(ring[-1], 'head', [(dev, (dev + 1) % 4) for dev in range(4)])]
    all_gather x2 -> x0, waiting for transfers between devices: 41.2 us -> none  [shards(): whole = lax.all_gather(normed, 'head', axis=0, tiled=True)]
    dot_general x2, matrix products: 12.2 us -> 25.7 us  [shards(): jnp.einsum('td,jdc->tjc', whole, lax.all_gather(attend_weight[layer], 'vi...]
  transfers between devices with their start and end apart: 10 -> 14, of which waited for: 7 -> 8; matrix products, arithmetic and copies ran while one was open for 36% -> 34% of each run, Pallas kernels for 0% -> 0%
where the time goes in v1:
time: 665 us; the launch traced here: 654 us
  matrix products  309 us (46%)
  waiting for transfers between devices  131 us (20%)
  blocking collectives  84.6 us (13%)
  local copies, waits for them, and re-layouts  54.2 us (8%)
  other arithmetic  49.9 us (8%)
  between operations  14.4 us (2%)
  starting transfers between devices  8.27 us (1%)
    all_gather x2, blocking collectives, shards(): full_fast = lax.all_gather(local_fast, 'view', axis=3, tiled=True)  84.6 us
    ppermute x6, waiting for transfers between devices, shards(): lax.ppermute(ring[-1], 'head', [(dev, (dev + 1) % 4) for dev in range(4)])  54.8 us
    psum x2, waiting for transfers between devices, shards(): lax.psum(gradients.astype(jnp.bfloat16), 'view').astype(jnp.float32)  47.3 us
    dot_general x8, matrix products, attend_block(): jnp.einsum('vhqk,vkhd->vqhd', probs, value_views, preferred_element_type=...  34.6 us
    dot_general x8, matrix products, fast_apply(): jnp.einsum('thf,hdf->thd', hidden, weights[:, 2], preferred_element_type=...  32.7 us
    dot_general x8, matrix products, attend_block(): jnp.einsum('vqhd,vkhd->vhqk', query_block, key_views, preferred_element_t...  32.4 us
    dot_general x8, matrix products, fast_apply(): jnp.einsum('thd,hdf->thf', queries, weights[:, 0], preferred_element_type...  29.2 us
    all_to_all x2, waiting for transfers between devices, shards(): lax.all_to_all(mixed, 'head', split_axis=0, concat_axis=1, tiled=True)  28.7 us
  transfers between devices with their start and end apart: 14, of which 8 were waited for; matrix products, arithmetic and copies ran while one was open for 34% of the time, Pallas kernels for 0%

profile of v1, /device:TPU:0, one launch (start us, length us, event | category | flops | bytes accessed | tf_op | source)
XLA Modules:
  0.0 653.7 jit_solution(12199085395694789830)
XLA Ops:
  11.7 12.8 %collective-permute-done = bf16[512,1024]{1,0:T(8,128)(2,1)S(1)} collective-permute-done((bf16[512,1024]{1,0:T(8,128)(2,1)S(1)}, bf16[512,1024]{1,0:T(8,128)(2,1)S(1)}, u32[]{:S(2)}, u32[]{:S(2)}) %collective-permute-start) | collective-permute-done | bytes 1048608 | tf_op jit(solution)/shard_map/ppermute | solution.py:69
  24.6 14.3 %collective-permute-done.1 = bf16[512,1024]{1,0:T(8,128)(2,1)} collective-permute-done((bf16[512,1024]{1,0:T(8,128)(2,1)S(1)}, bf16[512,1024]{1,0:T(8,128)(2,1)}, u32[]{:S(2)}, u32[]{:S(2)}) %collective-permute-start.1) | collective-permute-done | bytes 1048608 | tf_op jit(solution)/shard_map/ppermute | solution.py:69
  39.8 43.3 %all-gather.1 = bf16[1,4,3,64,512]{3,1,2,0,4:T(4,128)(2,1)} all-gather(bf16[1,4,3,64,64]{3,1,2,0,4:T(4,128)(2,1)S(1)} %copy.61), channel_id=3, replica_groups=mesh['view'=8,'head'=4] {'view'}, dimensions={4}, use_global_device_ids=true | all-gather | bytes 884736 | tf_op jit(solution)/shard_map/all_gather | solution.py:108
  87.0 12.9 %fusion.206 = bf16[2048,3,256]{0,2,1:T(8,128)(2,1)S(1)} fusion(s32[]{:T(128)S(6)} %select_n.13, bf16[512,1024]{1,0:T(8,128)(2,1)} %collective-permute-done.2, bf16[512,1024]{1,0:T(8,128)(2,1)} %collective-permute-done.1, bf16[512,1024]{1,0:T(8,128)(2,1)} %copy-done.22, bf16[512,1024]{1,0:T(8,128)(2,1)S(1)} %fusion.213, ...), kind=kOutput, calls=%fused_computation.218 | convolution fusion | flops 3256352768 | bytes 8912900 | tf_op jit(solution)/shard_map/td,jdc->tjc/dot_general | solution.py:75
  103.3 3.7 reshape.323
  114.2 60.3 %while.66 = (s32[]{:T(128)}, f32[4,3,64,512]{3,2,0,1:T(8,128)S(1)}, bf16[4,512,4,64]{1,3,2,0:T(8,128)(2,1)}, s32[4,512]{1,0:T(4,128)S(1)}, bf16[4,512,4,64]{1,3,...) while((s32[]{:T(128)}, f32[4,3,64,512]{3,2,0,1:T(8,128)S(1)}, ...), condition=%wide.region_7.9_spmd.clone, body=%wide.region_6.8_spmd.clone.sunk | while | flops 830996992 | bytes 50605152 | solution.py:115
  191.3 33.7 %while.62 = (s32[]{:T(128)}, f32[4,1,512,4,64]{2,4,3,1,0:T(8,128)}, bf16[4,1,512,4,64]{2,4,3,1,0:T(8,128)(2,1)}, bf16[1,2048,4,64]{1,3,2,0:T(8,128)(2,1)S(1)}, bf16[1,2048,4,64]{1,3,2,0:T(8,128)(2,1)}, /*index=5*/s32[]{:T(128)}) while((s32[]{:T(128)}, f32[4,1,512,4,64]{2,4,3,1,0:T(8,128)}, bf16[4,1,512,4,64]{2,4,3,1,0:T(8,128)(2,1)}, ...), condition=%wide.region_5.7_spmd, body=%wide.region_3.6_spmd.sunk | while | flops 1094711296 | bytes 40649824 | solution.py:104
  191.3 4.1 fusion.390
  195.5 4.3 fusion.391
  199.8 4.0 fusion.390
  203.8 4.3 fusion.391
  208.2 4.0 fusion.390
  212.2 4.3 fusion.391
  216.5 4.0 fusion.390
  220.6 4.3 fusion.391
  226.7 24.6 %all-reduce.3.cloned.1.call-done = bf16[4,3,64,512]{3,2,1,0:T(8,128)(2,1)} async-done(((bf16[4,3,64,512]{3,2,1,0:T(8,128)(2,1)}), bf16[4,3,64,512]{3,2,1,0:T(8,128)(2,1)}) %all-reduce.3.cloned.1.call-update) | async-done | bytes 786448 | tf_op jit(solution)/shard_map/psum | solution.py:120
  273.6 31.4 %while.63 = (s32[]{:T(128)}, f32[4,512,4,64]{1,3,2,0:T(8,128)S(1)}, bf16[4,512,4,64]{1,3,2,0:T(8,128)(2,1)}, bf16[4,3,64,512]{3,2,0,1:T(8,128)(2,1)S(1)}, s32[]{:T(128)}) while((s32[]{:T(128)}, f32[4,512,4,64]{1,3,2,0:T(8,128)S(1)}, bf16[4,512,4,64]{1,3,2,0:T(8,128)(2,1)}, bf16[4,3,64,512]{3,2,0,1:T(8,128)(2,1)S(1)}, s32[]{:T(128)}) %tuple.132), condition=%wide.region_12.14_spmd, body=%wide.region_10.13_spmd.sunk | while | flops 409339904 | bytes 11306049 | solution.py:130
  273.6 3.6 fusion.396
  277.2 4.1 multiply_reduce_fusion.8
  285.0 4.1 multiply_reduce_fusion.8
  292.9 4.1 multiply_reduce_fusion.8
  300.8 4.1 multiply_reduce_fusion.8
  308.0 3.6 all-to-all-start
  311.7 14.3 %all-to-all-done = bf16[4,512,256]{1,2,0:T(8,128)(2,1)S(1)} async-done(((bf16[4,512,256]{1,2,0:T(8,128)(2,1)}), bf16[4,512,256]{1,2,0:T(8,128)(2,1)S(1)}, u32[]{:S(2)}, u32[]{:S(2)}) %all-to-all-start) | async-done | bytes 1048608 | tf_op jit(solution)/shard_map/all_to_all | solution.py:134
  331.2 13.3 %collective-permute-done.3 = bf16[512,1024]{1,0:T(8,128)(2,1)S(1)} collective-permute-done((bf16[512,1024]{1,0:T(8,128)(2,1)S(1)}, bf16[512,1024]{1,0:T(8,128)(2,1)S(1)}, u32[]{:S(2)}, u32[]{:S(2)}) %collective-permute-start.3) | collective-permute-done | bytes 1048608 | tf_op jit(solution)/shard_map/ppermute | solution.py:69
  344.5 14.3 %collective-permute-done.4 = bf16[512,1024]{1,0:T(8,128)(2,1)} collective-permute-done((bf16[512,1024]{1,0:T(8,128)(2,1)S(1)}, bf16[512,1024]{1,0:T(8,128)(2,1)}, u32[]{:S(2)}, u32[]{:S(2)}) %collective-permute-start.4) | collective-permute-done | bytes 1048608 | tf_op jit(solution)/shard_map/ppermute | solution.py:69
  359.2 41.4 %all-gather.4 = bf16[1,4,3,64,512]{3,1,2,0,4:T(4,128)(2,1)} all-gather(bf16[1,4,3,64,64]{3,1,2,0,4:T(4,128)(2,1)S(1)} %copy.63), channel_id=6, replica_groups=mesh['view'=8,'head'=4] {'view'}, dimensions={4}, use_global_device_ids=true | all-gather | bytes 884736 | tf_op jit(solution)/shard_map/all_gather | solution.py:108
  403.2 12.9 %fusion.209 = bf16[2048,3,256]{0,2,1:T(8,128)(2,1)S(1)} fusion(s32[]{:T(128)S(6)} %select_n.13, bf16[512,1024]{1,0:T(8,128)(2,1)} %collective-permute-done.5, bf16[512,1024]{1,0:T(8,128)(2,1)} %collective-permute-done.4, bf16[512,1024]{1,0:T(8,128)(2,1)} %copy-done.23, bf16[512,1024]{1,0:T(8,128)(2,1)S(1)} %fusion.216, ...), kind=kOutput, calls=%fused_computation.219 | convolution fusion | flops 3256352768 | bytes 8912900 | tf_op jit(solution)/shard_map/td,jdc->tjc/dot_general | solution.py:75
  419.3 3.7 reshape.327
  430.3 63.1 %while.67 = (s32[]{:T(128)}, f32[4,3,64,512]{3,2,0,1:T(8,128)S(1)}, bf16[4,512,4,64]{1,3,2,0:T(8,128)(2,1)}, s32[4,512]{1,0:T(4,128)}, bf16[4,512,4,64]{1,3,2,0:...) while((s32[]{:T(128)}, f32[4,3,64,512]{3,2,0,1:T(8,128)S(1)}, ...), condition=%wide.region_20.22_spmd.clone, body=%wide.region_19.21_spmd.clone.sunk | while | flops 830996992 | bytes 50605152 | solution.py:115
  509.9 33.9 %while.64 = (s32[]{:T(128)}, f32[4,1,512,4,64]{2,4,3,1,0:T(8,128)}, bf16[4,1,512,4,64]{2,4,3,1,0:T(8,128)(2,1)}, bf16[1,2048,4,64]{1,3,2,0:T(8,128)(2,1)S(1)}, bf16[1,2048,4,64]{1,3,2,0:T(8,128)(2,1)}, /*index=5*/s32[]{:T(128)}) while((s32[]{:T(128)}, f32[4,1,512,4,64]{2,4,3,1,0:T(8,128)}, bf16[4,1,512,4,64]{2,4,3,1,0:T(8,128)(2,1)}, ...), condition=%wide.region_18.20_spmd, body=%wide.region_16.19_spmd.sunk | while | flops 1094711296 | bytes 40649824 | solution.py:104
  509.9 4.1 fusion.398
  514.0 4.3 fusion.399
  518.3 4.0 fusion.398
  522.3 4.3 fusion.399
  526.7 4.0 fusion.398
  530.7 4.3 fusion.399
  535.0 4.0 fusion.398
  539.1 4.3 fusion.399
  545.5 22.8 %all-reduce.5.cloned.1.call-done = bf16[4,3,64,512]{3,2,1,0:T(8,128)(2,1)} async-done(((bf16[4,3,64,512]{3,2,1,0:T(8,128)(2,1)}), bf16[4,3,64,512]{3,2,1,0:T(8,128)(2,1)}) %all-reduce.5.cloned.1.call-update) | async-done | bytes 786448 | tf_op jit(solution)/shard_map/psum | solution.py:120
  590.3 31.3 %while.65 = (s32[]{:T(128)}, f32[4,512,4,64]{1,3,2,0:T(8,128)S(1)}, bf16[4,512,4,64]{1,3,2,0:T(8,128)(2,1)}, bf16[4,3,64,512]{3,2,0,1:T(8,128)(2,1)S(1)}, s32[]{:T(128)}) while((s32[]{:T(128)}, f32[4,512,4,64]{1,3,2,0:T(8,128)S(1)}, bf16[4,512,4,64]{1,3,2,0:T(8,128)(2,1)}, bf16[4,3,64,512]{3,2,0,1:T(8,128)(2,1)S(1)}, s32[]{:T(128)}) %tuple.141), condition=%wide.region_25.27_spmd, body=%wide.region_23.26_spmd.sunk | while | flops 409339904 | bytes 11306049 | solution.py:130
  594.0 4.1 multiply_reduce_fusion.9
  601.8 4.1 multiply_reduce_fusion.9
  609.6 4.1 multiply_reduce_fusion.9
  617.5 4.1 multiply_reduce_fusion.9
  624.8 3.6 all-to-all-start.1
  628.4 14.4 %all-to-all-done.1 = bf16[4,512,256]{1,2,0:T(8,128)(2,1)S(1)} async-done(((bf16[4,512,256]{1,2,0:T(8,128)(2,1)}), bf16[4,512,256]{1,2,0:T(8,128)(2,1)S(1)}, u32[]{:S(2)}, u32[]{:S(2)}) %all-to-all-start.1) | async-done | bytes 1048608 | tf_op jit(solution)/shard_map/all_to_all | solution.py:134
  642.8 3.8 fusion.217
  (268 shorter events, 274.7 us)
Async XLA Ops:
  6.5 3.6 copy-start.18
  6.5 32.4 %copy-start.19 = (bf16[2,4,3,64,64]{4,3,2,1,0:T(8,128)(2,1)S(1)}, bf16[2,4,3,64,64]{4,3,2,1,0:T(8,128)(2,1)}, u32[]{:S(2)}) copy-start(bf16[2,4,3,64,64]{4,3,2,1,0:T(8,128)(2,1)} %param.22) | copy-start | bytes 589828
  6.5 80.4 %all-gather.11.cloned.1.call-start = ((), (), s32[]{:S(2)}) async-start(), calls=%async_computation.4 | async-start | bytes 1769472 | tf_op jit(solution)/shard_map/all_gather | solution.py:78
  9.6 15.0 %collective-permute-start = (bf16[512,1024]{1,0:T(8,128)(2,1)S(1)}, bf16[512,1024]{1,0:T(8,128)(2,1)S(1)}, u32[]{:S(2)}, u32[]{:S(2)}) collective-permute-start(bf16[512,1024]{1,0:T(8,128)(2,1)S(1)} %fusion.213), channel_id=1, source_target_pairs={{0,1},{1,2},{2,3},{3,0},{4,5},{5,6},{6,7},{7,4},{8,9},{9,10},{10,1... | collective-permute-start | bytes 3145736 | tf_op jit(solution)/shard_map/ppermute | solution.py:69
  11.7 239.5 %all-reduce.3.cloned.1.call-start = ((), (), s32[]{:S(2)}) async-start(), calls=%async_computation.2 | async-start | bytes 1572864 | tf_op jit(solution)/shard_map/psum | solution.py:120
  24.6 14.3 %copy-start.22 = (bf16[512,1024]{1,0:T(8,128)(2,1)}, bf16[512,1024]{1,0:T(8,128)(2,1)S(1)}, u32[]{:S(2)}) copy-start(bf16[512,1024]{1,0:T(8,128)(2,1)S(1)} %collective-permute-done) | copy-start | bytes 3145732
  24.6 14.3 %collective-permute-start.1 = (bf16[512,1024]{1,0:T(8,128)(2,1)S(1)}, bf16[512,1024]{1,0:T(8,128)(2,1)}, u32[]{:S(2)}, u32[]{:S(2)}) collective-permute-start(bf16[512,1024]{1,0:T(8,128)(2,1)S(1)} %collective-permute-done), channel_id=1, source_target_pairs={{0,1},{1,2},{2,3},{3,0},{4,5},{5,6},{6,7},{7,4},{8,9},{9,10},{10,1... | collective-permute-start | bytes 3145736 | tf_op jit(solution)/shard_map/ppermute | solution.py:69
  38.9 48.1 %collective-permute-start.2 = (bf16[512,1024]{1,0:T(8,128)(2,1)}, bf16[512,1024]{1,0:T(8,128)(2,1)}, u32[]{:S(2)}, u32[]{:S(2)}) collective-permute-start(bf16[512,1024]{1,0:T(8,128)(2,1)} %collective-permute-done.1), channel_id=1, source_target_pairs={{0,1},{1,2},{2,3},{3,0},{4,5},{5,6},{6,7},{7,4},{8,9},{9,10},{10,1... | collective-permute-start | bytes 3145736 | tf_op jit(solution)/shard_map/ppermute | solution.py:69
  39.8 46.5 %copy-start.21 = (s32[1,2048]{1,0:T(1,128)S(1)}, s32[1,2048]{1,0:T(1,128)}, u32[]{:S(2)}) copy-start(s32[1,2048]{1,0:T(1,128)} %param.23) | copy-start | bytes 24580
  99.9 3.3 copy-start.2
  174.5 2.0 copy-start.20
  174.5 1.1 copy-start.17
  175.6 136.1 %all-gather.13.cloned.1.call-start = ((), (), s32[]{:S(2)}) async-start(), calls=%async_computation.5 | async-start | bytes 2359296 | tf_op jit(solution)/shard_map/all_gather | solution.py:137
  176.5 5.0 copy-start
  191.3 33.8 %copy-start.5 = (f32[4,512,4,64]{1,0,3,2:T(4,128)S(1)}, f32[4,512,4,64]{1,0,3,2:T(4,128)}, u32[]{:S(2)}) copy-start(f32[4,512,4,64]{1,0,3,2:T(4,128)} %reshape.322) | copy-start | bytes 6291460
  191.3 4.1 copy-start.11
  199.8 4.0 copy-start.11
  208.2 4.0 copy-start.11
  216.5 4.0 copy-start.11
  251.2 5.2 copy-start.9
  269.5 2.1 copy-start.8
  308.0 18.1 %copy-start.6 = (bf16[512,1024]{1,0:T(8,128)(2,1)S(1)}, bf16[512,1024]{1,0:T(8,128)(2,1)}, u32[]{:S(2)}) copy-start(bf16[512,1024]{1,0:T(8,128)(2,1)} %param.19) | copy-start | bytes 3145732
  308.0 18.1 %all-to-all-start = ((bf16[4,512,256]{1,2,0:T(8,128)(2,1)}), bf16[4,512,256]{1,2,0:T(8,128)(2,1)S(1)}, u32[]{:S(2)}, u32[]{:S(2)}) async-start(bf16[4,512,256]{1,2,0:T(8,128)(2,1)} %fusion.224), calls=%async_computation | async-start | bytes 2097152 | tf_op jit(solution)/shard_map/all_to_all | solution.py:134
  311.6 91.5 %all-gather.15.cloned.1.call-start = ((), (), s32[]{:S(2)}) async-start(), calls=%async_computation.6 | async-start | bytes 1769472 | tf_op jit(solution)/shard_map/all_gather | solution.py:78
  329.0 1.0 copy-start.13
  329.0 1.3 copy-start.15
  329.0 30.0 %copy-start.16 = (bf16[1,4,3,64,64]{4,3,2,1,0:T(8,128)(2,1)S(1)}, bf16[1,4,3,64,64]{4,3,2,1,0:T(8,128)(2,1)}, u32[]{:S(2)}) copy-start(bf16[1,4,3,64,64]{4,3,2,1,0:T(8,128)(2,1)} %get-tuple-element.358) | copy-start | bytes 294916
  330.2 14.3 %collective-permute-start.3 = (bf16[512,1024]{1,0:T(8,128)(2,1)S(1)}, bf16[512,1024]{1,0:T(8,128)(2,1)S(1)}, u32[]{:S(2)}, u32[]{:S(2)}) collective-permute-start(bf16[512,1024]{1,0:T(8,128)(2,1)S(1)} %fusion.216), channel_id=1, source_target_pairs={{0,1},{1,2},{2,3},{3,0},{4,5},{5,6},{6,7},{7,4},{8,9},{9,10},{10,1... | collective-permute-start | bytes 3145736 | tf_op jit(solution)/shard_map/ppermute | solution.py:69
  331.1 237.1 %all-reduce.5.cloned.1.call-start = ((), (), s32[]{:S(2)}) async-start(), calls=%async_computation.3 | async-start | bytes 1572864 | tf_op jit(solution)/shard_map/psum | solution.py:120
  344.5 14.3 %copy-start.23 = (bf16[512,1024]{1,0:T(8,128)(2,1)}, bf16[512,1024]{1,0:T(8,128)(2,1)S(1)}, u32[]{:S(2)}) copy-start(bf16[512,1024]{1,0:T(8,128)(2,1)S(1)} %collective-permute-done.3) | copy-start | bytes 3145732
  344.5 14.3 %collective-permute-start.4 = (bf16[512,1024]{1,0:T(8,128)(2,1)S(1)}, bf16[512,1024]{1,0:T(8,128)(2,1)}, u32[]{:S(2)}, u32[]{:S(2)}) collective-permute-start(bf16[512,1024]{1,0:T(8,128)(2,1)S(1)} %collective-permute-done.3), channel_id=1, source_target_pairs={{0,1},{1,2},{2,3},{3,0},{4,5},{5,6},{6,7},{7,4},{8,9},{9,10},{10,1... | collective-permute-start | bytes 3145736 | tf_op jit(solution)/shard_map/ppermute | solution.py:69
  358.8 44.3 %collective-permute-start.5 = (bf16[512,1024]{1,0:T(8,128)(2,1)}, bf16[512,1024]{1,0:T(8,128)(2,1)}, u32[]{:S(2)}, u32[]{:S(2)}) collective-permute-start(bf16[512,1024]{1,0:T(8,128)(2,1)} %collective-permute-done.4), channel_id=1, source_target_pairs={{0,1},{1,2},{2,3},{3,0},{4,5},{5,6},{6,7},{7,4},{8,9},{9,10},{10,1... | collective-permute-start | bytes 3145736 | tf_op jit(solution)/shard_map/ppermute | solution.py:69
  416.1 3.2 copy-start.3
  494.4 134.0 %all-gather.17.cloned.1.call-start = ((), (), s32[]{:S(2)}) async-start(), calls=%async_computation.7 | async-start | bytes 2359296 | tf_op jit(solution)/shard_map/all_gather | solution.py:137
  495.0 5.0 copy-start.1
  509.9 33.9 %copy-start.4 = (f32[4,512,4,64]{1,0,3,2:T(4,128)S(1)}, f32[4,512,4,64]{1,0,3,2:T(4,128)}, u32[]{:S(2)}) copy-start(f32[4,512,4,64]{1,0,3,2:T(4,128)} %reshape.326) | copy-start | bytes 6291460
  509.9 4.1 copy-start.12
  518.3 4.0 copy-start.12
  526.7 4.0 copy-start.12
  535.0 4.0 copy-start.12
  568.2 5.2 copy-start.10
  586.3 2.1 copy-start.7
  624.8 18.1 %copy-start.14 = (bf16[512,1024]{1,0:T(8,128)(2,1)S(1)}, bf16[512,1024]{1,0:T(8,128)(2,1)}, u32[]{:S(2)}) copy-start(bf16[512,1024]{1,0:T(8,128)(2,1)} %copy-done.13) | copy-start | bytes 3145732
  624.8 18.1 %all-to-all-start.1 = ((bf16[4,512,256]{1,2,0:T(8,128)(2,1)}), bf16[4,512,256]{1,2,0:T(8,128)(2,1)S(1)}, u32[]{:S(2)}, u32[]{:S(2)}) async-start(bf16[4,512,256]{1,2,0:T(8,128)(2,1)} %fusion.220), calls=%async_computation.1 | async-start | bytes 2097152 | tf_op jit(solution)/shard_map/all_to_all | solution.py:134
Sparse Core Ops, SparseCore 0:
  11.8 59.8 all-gather.10
  175.7 75.5 all-reduce.2
  253.4 48.2 all-gather.12
  331.3 55.7 all-gather.14
  494.5 73.6 all-reduce.4
  570.2 48.2 all-gather.16
